TPU v7x, 32 devices: a whole 2x2x4 slice. The times are simulated.
32 devices in a mesh: freq: 4 (over x, core), rcv: 8 (over z, y).
Axes of the slice: x: 2, y: 2, z: 4, core: 2. Of those that a mesh axis runs over, the one named last changes fastest.
Arguments:
- reflection: bfloat16 [8, 2, 2560, 2560], P('freq', None, 'rcv'), may hold values from -5 to 5, as said below
- starts: int32 [2560, 192], P('rcv'), may hold values from 8 to 56
- focusing: float32 [8, 2560, 2, 192], P('freq', 'rcv'), may hold values from -6 to 6
- residual: float32 [8, 2560, 2, 192], P('freq', 'rcv'), may hold values from -6 to 6
- direction: float32 [8, 2560, 2, 192], P('freq', 'rcv'), may hold values from -6 to 6
- gradient: float32 [8, 2560, 2, 192], P('freq', 'rcv'), may hold values from -30 to 30
Outputs:
- new_focusing: float32 [8, 2560, 2, 192], P('freq', 'rcv')
- new_residual: float32 [8, 2560, 2, 192], P('freq', 'rcv')
- new_direction: float32 [8, 2560, 2, 192], P('freq', 'rcv')
- green_field: float32 [8, 2560, 2, 192], P('freq', 'rcv')
- focal_correlation: float32 [8, 2, 192], P('freq')
Inputs may be any that keep to these rules, and one draw needn't show every extreme that they name: Each frequency's matrix is symmetric in source and receiver: reflection[f, c, s, r] = reflection[f, c, r, s].
All inputs are finite; a program needn't handle non-finite values.
Results may differ from a plain program's by a relative error of at most 0.0003.
The roundings to bfloat16 on the way count: a program that leaves them out, or rounds other values in their place, can miss the bound.
Values may be sent and summed in bfloat16 or wider, within the bound.
No kernel may reach another device: no remote copies, remote signals or barrier semaphores. Data moves between devices by JAX's collectives and lax.ppermute only.
A program may use at most 64 MiB of HBM per device.

v0:
```python
import math
import jax
import jax.numpy as jnp
from jax import lax
from jax.sharding import PartitionSpec as P

N = 2560
F = 8
TS = 64
band_start = 5
tiny = 1e-06
highest = lax.Precision.HIGHEST


def tables(count):
    times = jnp.arange(TS, dtype=jnp.float32)[:, None]
    bins = (jnp.arange(count, dtype=jnp.int32) + band_start).astype(jnp.float32)[None, :]
    phase = 2.0 * jnp.pi * times * bins / TS
    return (jnp.cos(phase), jnp.sin(phase))


def contract_time(table, values):
    return jnp.einsum("tf,frk->trk", table, values, precision=highest)


def contract_back(table, values):
    return jnp.einsum("tf,trk->frk", table, values, precision=highest)


def time_gate(field, forward_cos, forward_sin, back_cos, back_sin, limits, complement):
    real_part = field[:, :, 0]
    imag_part = field[:, :, 1]
    time_real = contract_time(forward_cos, real_part) - contract_time(forward_sin, imag_part)
    time_imag = contract_time(forward_sin, real_part) + contract_time(forward_cos, imag_part)
    clock = jnp.arange(TS, dtype=jnp.int32)[:, None, None]
    window = (clock < limits[None]).astype(jnp.float32)
    if complement:
        window = 1.0 - window
    kept_real = window * time_real
    kept_imag = window * time_imag
    out_real = (contract_back(back_cos, kept_real) + contract_back(back_sin, kept_imag)) / TS
    out_imag = (contract_back(back_cos, kept_imag) - contract_back(back_sin, kept_real)) / TS
    return jnp.stack([out_real, out_imag], axis=2)


def combine(total, conjugate):
    if conjugate:
        out_real = total[:, 0, :, 0] + total[:, 1, :, 1]
        out_imag = total[:, 0, :, 1] - total[:, 1, :, 0]
    else:
        out_real = total[:, 0, :, 0] - total[:, 1, :, 1]
        out_imag = total[:, 0, :, 1] + total[:, 1, :, 0]
    return jnp.stack([out_real, out_imag], axis=2)


def per_device(reflection, starts, focusing, residual, direction, gradient):
    local_rows = reflection.shape[2]
    groups = lax.axis_size("freq")
    position = lax.axis_index("freq")
    cos_table, sin_table = tables(F)

    def gate(field, complement):
        spread = lax.all_to_all(field, "freq", split_axis=1, concat_axis=0, tiled=True)
        share = local_rows // groups
        limits = lax.dynamic_slice_in_dim(starts, position * share, share, 0)
        gated_part = time_gate(
            spread, cos_table, sin_table, cos_table, sin_table, limits, complement
        )
        return lax.all_to_all(gated_part, "freq", split_axis=0, concat_axis=1, tiled=True)

    def accumulate(piece):
        return jnp.einsum("fpnm,fmqk->fpnqk", reflection, piece, preferred_element_type=jnp.float32)

    direction_low = direction.astype(jnp.bfloat16)
    focusing_low = focusing.astype(jnp.bfloat16)
    aimed_total = accumulate(lax.all_gather(direction_low, "rcv", axis=1, tiled=True))
    direction_image = combine(aimed_total, False)
    gamma = lax.psum(jnp.sum(gradient * gradient), ("freq", "rcv"))
    image = gate(direction_image, False)
    curvature = lax.psum(jnp.sum(image * image), ("freq", "rcv"))
    alpha = gamma / (curvature + tiny)
    new_focusing = focusing + alpha * direction
    new_residual = residual - alpha * image
    gated = gate(new_residual, False).astype(jnp.bfloat16)
    total = accumulate(lax.all_gather(gated, "rcv", axis=1, tiled=True))
    new_gradient = combine(total, True)
    new_gamma = lax.psum(jnp.sum(new_gradient * new_gradient), ("freq", "rcv"))
    new_direction = new_gradient + new_gamma / (gamma + tiny) * direction
    focus_total = accumulate(lax.all_gather(focusing_low, "rcv", axis=1, tiled=True))
    focusing_image = combine(focus_total, False)
    green_field = gate(focusing_image + alpha * direction_image, True)
    corr_real = jnp.sum(
        green_field[:, :, 0] * new_focusing[:, :, 0] + green_field[:, :, 1] * new_focusing[:, :, 1],
        axis=1,
    )
    corr_imag = jnp.sum(
        green_field[:, :, 1] * new_focusing[:, :, 0] - green_field[:, :, 0] * new_focusing[:, :, 1],
        axis=1,
    )
    partial_corr = jnp.stack([corr_real, corr_imag], axis=1)
    focal_correlation = lax.psum(partial_corr, "rcv") / math.sqrt(N)
    return (new_focusing, new_residual, new_direction, green_field, focal_correlation)


def solution(mesh):
    return jax.shard_map(
        per_device,
        mesh=mesh,
        in_specs=(
            P("freq", None, "rcv", None),
            P("rcv", None),
            P("freq", "rcv", None, None),
            P("freq", "rcv", None, None),
            P("freq", "rcv", None, None),
            P("freq", "rcv", None, None),
        ),
        out_specs=(
            P("freq", "rcv", None, None),
            P("freq", "rcv", None, None),
            P("freq", "rcv", None, None),
            P("freq", "rcv", None, None),
            P("freq", None, None),
        ),
        check_vma=False,
    )
```

profile of v0, /device:TPU:0, one launch (start us, length us, event | category | flops | bytes accessed | tf_op | source)
XLA Modules:
  0.0 475.7 jit_solution(8466674727431938095)
XLA Ops:
  10.4 89.0 %all-gather.4.cloned.1.call-done = bf16[2,2560,2,192]{3,2,0,1:T(2,128)(2,1)} async-done(((bf16[2,320,2,192]{3,2,0,1:T(2,128)(2,1)}), bf16[2,2560,2,192]{3,2,0,1:T(2,128)(2,1)}) %all-gather.4.cloned.1.call-update) | async-done | bytes 3932176 | tf_op jit(solution)/shard_map/all_gather | solution.py:76
  99.4 8.1 %fusion.2 = f32[2,2,320,2,192]{2,4,3,1,0:T(8,128)S(1)} fusion(bf16[2,2,320,2560]{3,2,1,0:T(8,128)(2,1)} %param.6, bf16[2,2560,2,192,1]{3,2,0,1,4:T(2,128)(2,1)} %bitcast.192), kind=kOutput, calls=%fused_computation.2 | convolution fusion | flops 2516582400 | bytes 12451840 | tf_op jit(solution)/shard_map/fpnm,fmqk->fpnqk/dot_general | solution.py:72
  107.7 2.0 copy.107
  109.7 3.5 all-to-all-start
  114.6 2.2 copy.125
  117.2 13.3 %all-to-all-done = f32[2,320,2,192]{3,0,2,1:T(2,128)S(1)} async-done(((f32[2,320,2,192]{3,0,2,1:T(2,128)}), f32[2,320,2,192]{3,0,2,1:T(2,128)S(1)}, u32[]{:S(2)}, u32[]{:S(2)}) %all-to-all-start) | async-done | bytes 983072 | tf_op jit(solution)/shard_map/all_to_all | solution.py:63
  132.6 4.4 fusion.27
  137.1 4.4 fusion.26
  141.5 5.0 %subtract_select_fusion.1 = f32[64,80,192]{2,0,1:T(8,128)S(1)} fusion(f32[64,80,192]{2,0,1:T(8,128)S(1)} %fusion.27, s32[80,192]{1,0:T(8,128)S(1)} %copy.102, f32[8,80,2,192]{3,0,1,2:T(8,128)S(1)} %all_to_all.69, f32[8]{0:T(128)S(1)} %add_convert_fusion, f32[64]{0:T(128)S(1)} %iota_multiply_fusion), kind=kOutput, calls=%fused_computation.15 | convolution fusion | flops 97321984 | bytes 9913344 | tf_op jit(solution)/shard_map/tf,frk->trk/dot_general | solution.py:23
  146.6 2.6 fusion.67
  149.2 4.9 %add_select_fusion.1 = f32[64,80,192]{2,0,1:T(8,128)S(1)} fusion(f32[64,80,192]{2,0,1:T(8,128)S(1)} %fusion.26, s32[80,192]{1,0:T(8,128)S(1)} %copy.102, f32[8,80,2,192]{3,0,1,2:T(8,128)S(1)} %all_to_all.69, f32[8]{0:T(128)S(1)} %add_convert_fusion, f32[64]{0:T(128)S(1)} %iota_multiply_fusion), kind=kOutput, calls=%fused_computation.14 | convolution fusion | flops 97321984 | bytes 9913344 | tf_op jit(solution)/shard_map/tf,frk->trk/dot_general | solution.py:23
  154.1 2.9 fusion.25
  156.9 2.6 fusion.64
  159.6 2.7 fusion.23
  163.8 3.5 all-to-all-start.1
  168.3 16.2 %all-to-all-done.1 = f32[8,80,2,192]{3,1,2,0:T(8,128)S(1)} async-done(((f32[8,80,2,192]{3,1,2,0:T(8,128)}), f32[8,80,2,192]{3,1,2,0:T(8,128)S(1)}, u32[]{:S(2)}, u32[]{:S(2)}) %all-to-all-start.1) | async-done | bytes 983072 | tf_op jit(solution)/shard_map/all_to_all | solution.py:69
  187.2 38.8 %all-reduce = (f32[]{:T(128)}, f32[]{:T(128)}) all-reduce(f32[]{:T(128)} %multiply_reduce_fusion.2, f32[]{:T(128)} %multiply_reduce_fusion), channel_id=1, replica_groups=mesh['freq'=4,'rcv'=8] {'freq','rcv'}, use_global_device_ids=true, to_apply=%region_1.0 | all-reduce | flops 2 | bytes 16 | tf_op jit(solution)/shard_map/psum | solution.py:78
  228.7 20.6 %all_to_all.90 = f32[2,320,2,192]{3,2,0,1:T(2,128)S(1)} all-to-all(f32[2,320,2,192]{3,2,0,1:T(2,128)S(1)} %copy.115), channel_id=1, replica_groups=mesh['freq'=4,'rcv'=8] {'freq'}, dimensions={1} | all-to-all | bytes 1966080 | tf_op jit(solution)/shard_map/all_to_all | solution.py:63
  249.6 2.1 copy.117
  251.7 2.6 all_to_all.74
  254.2 4.4 fusion.29
  258.7 4.4 fusion.28
  263.1 5.0 %subtract_select_fusion = f32[64,80,192]{2,0,1:T(8,128)S(1)} fusion(f32[64,80,192]{2,0,1:T(8,128)S(1)} %fusion.29, s32[80,192]{1,0:T(8,128)S(1)} %copy.102, f32[8,80,2,192]{3,0,1,2:T(8,128)S(1)} %all_to_all.74, f32[8]{0:T(128)S(1)} %add_convert_fusion, f32[64]{0:T(128)S(1)} %iota_multiply_fusion), kind=kOutput, calls=%fused_computation.13 | convolution fusion | flops 97321984 | bytes 9913344 | tf_op jit(solution)/shard_map/tf,frk->trk/dot_general | solution.py:23
  268.2 2.6 fusion.61
  270.8 4.9 %add_select_fusion = f32[64,80,192]{2,0,1:T(8,128)S(1)} fusion(f32[64,80,192]{2,0,1:T(8,128)S(1)} %fusion.28, s32[80,192]{1,0:T(8,128)S(1)} %copy.102, f32[8,80,2,192]{3,0,1,2:T(8,128)S(1)} %all_to_all.74, f32[8]{0:T(128)S(1)} %add_convert_fusion, f32[64]{0:T(128)S(1)} %iota_multiply_fusion), kind=kOutput, calls=%fused_computation.12 | convolution fusion | flops 97321984 | bytes 9913344 | tf_op jit(solution)/shard_map/tf,frk->trk/dot_general | solution.py:23
  275.7 2.6 fusion.21
  278.3 2.8 fusion.58
  281.1 2.6 fusion.19
  284.0 12.6 %all_to_all.91 = bf16[8,80,2,192]{3,1,2,0:T(8,128)(2,1)S(1)} all-to-all(bf16[8,80,2,192]{3,1,2,0:T(8,128)(2,1)S(1)} %copy.118), channel_id=1, replica_groups=mesh['freq'=4,'rcv'=8] {'freq'}, dimensions={0} | all-to-all | bytes 983040 | tf_op jit(solution)/shard_map/all_to_all | solution.py:69
  298.3 8.2 %fusion.4 = f32[2,2,320,2,192]{2,4,0,3,1:T(8,128)S(1)} fusion(bf16[2,2560,2,192,1]{3,2,0,1,4:T(2,128)(2,1)} %bitcast.190, bf16[2,2,320,2560]{3,2,1,0:T(8,128)(2,1)} %param.6), kind=kOutput, calls=%fused_computation.4 | convolution fusion | flops 2516582400 | bytes 12451840 | tf_op jit(solution)/shard_map/fpnm,fmqk->fpnqk/dot_general | solution.py:72
  307.8 2.6 copy.131
  310.4 19.7 %all_to_all.92 = f32[2,320,2,192]{3,0,2,1:T(2,128)S(1)} all-to-all(f32[2,320,2,192]{3,0,2,1:T(2,128)S(1)} %copy.131), channel_id=1, replica_groups=mesh['freq'=4,'rcv'=8] {'freq'}, dimensions={1} | all-to-all | bytes 1966080 | tf_op jit(solution)/shard_map/all_to_all | solution.py:63
  330.3 2.1 copy.133
  332.4 2.6 all_to_all.79
  335.0 4.4 fusion.31
  339.4 4.4 fusion.30
  343.8 5.4 %subtract_multiply_fusion = f32[64,80,192]{2,0,1:T(8,128)S(1)} fusion(f32[64,80,192]{2,0,1:T(8,128)S(1)} %fusion.31, s32[80,192]{1,0:T(8,128)S(1)} %copy.102, f32[8,80,2,192]{3,0,1,2:T(8,128)S(1)} %all_to_all.79, f32[8]{0:T(128)S(1)} %add_convert_fusion, f32[64]{0:T(128)S(1)} %iota_multiply_fusion), kind=kOutput, calls=%fused_computation.10 | convolution fusion | flops 99288064 | bytes 9913344 | tf_op jit(solution)/shard_map/tf,frk->trk/dot_general | solution.py:23
  349.3 2.6 fusion.55
  351.9 5.2 %add_multiply_fusion = f32[64,80,192]{2,0,1:T(8,128)S(1)} fusion(f32[64,80,192]{2,0,1:T(8,128)S(1)} %fusion.30, s32[80,192]{1,0:T(8,128)S(1)} %copy.102, f32[8,80,2,192]{3,0,1,2:T(8,128)S(1)} %all_to_all.79, f32[8]{0:T(128)S(1)} %add_convert_fusion, f32[64]{0:T(128)S(1)} %iota_multiply_fusion), kind=kOutput, calls=%fused_computation.9 | convolution fusion | flops 99288064 | bytes 9913344 | tf_op jit(solution)/shard_map/tf,frk->trk/dot_general | solution.py:23
  357.2 2.6 fusion.17
  359.8 2.8 fusion.52
  362.6 2.7 fusion.15
  366.9 3.5 all-to-all-start.5
  372.5 15.1 %all-to-all-done.5 = f32[8,80,2,192]{3,1,2,0:T(8,128)S(1)} async-done(((f32[8,80,2,192]{3,1,2,0:T(8,128)}), f32[8,80,2,192]{3,1,2,0:T(8,128)S(1)}, u32[]{:S(2)}, u32[]{:S(2)}) %all-to-all-start.5) | async-done | bytes 983072 | tf_op jit(solution)/shard_map/all_to_all | solution.py:69
  390.4 10.1 %fusion.9 = f32[2,2,320,2,192]{2,4,1,3,0:T(8,128)S(1)} fusion(bf16[2,2,320,2560]{3,2,1,0:T(8,128)(2,1)} %param.6, bf16[2,2560,2,192,1]{3,2,0,1,4:T(2,128)(2,1)} %bitcast.191), kind=kOutput, calls=%fused_computation.17 | convolution fusion | flops 2516582400 | bytes 12451840 | tf_op jit(solution)/shard_map/fpnm,fmqk->fpnqk/dot_general | solution.py:72
  402.7 39.1 %psum.30 = f32[]{:T(128)} all-reduce(f32[]{:T(128)} %multiply_reduce_fusion.1), channel_id=1, replica_groups=mesh['freq'=4,'rcv'=8] {'freq','rcv'}, use_global_device_ids=true, to_apply=%region_5.0 | all-reduce | flops 1 | bytes 8 | tf_op jit(solution)/shard_map/psum | solution.py:87
  442.5 2.5 multiply_add_fusion
  446.5 20.7 %psum.31 = f32[2,2,192]{2,0,1:T(2,128)S(1)} all-reduce(f32[2,2,192]{2,0,1:T(2,128)S(1)} %pad_maximum_fusion.5), channel_id=1, replica_groups=mesh['freq'=4,'rcv'=8] {'rcv'}, use_global_device_ids=true, to_apply=%region_8.0 | all-reduce | flops 768 | bytes 6144 | tf_op jit(solution)/shard_map/psum | solution.py:101
  (73 shorter events, 28.5 us)
Async XLA Ops:
  7.2 109.8 %copy-start = (s32[320,192]{0,1:T(8,128)S(1)}, s32[320,192]{0,1:T(8,128)}, u32[]{:S(2)}) copy-start(s32[320,192]{0,1:T(8,128)} %param.7) | copy-start | bytes 737284
  7.2 92.2 %all-gather.4.cloned.1.call-start = ((), (), s32[]{:S(2)}) async-start(), calls=%async_computation.6 | async-start | bytes 5898240 | tf_op jit(solution)/shard_map/all_gather | solution.py:76
  107.6 9.2 %copy-start.2 = (f32[2,320,1,192]{1,3,0,2:T(8,128)}, f32[2,320,1,192]{1,3,0,2:T(8,128)S(1)}, u32[]{:S(2)}) copy-start(f32[2,320,1,192]{1,3,0,2:T(8,128)S(1)} %fusion.39) | copy-start | bytes 1474564
  109.7 20.8 %all-to-all-start = ((f32[2,320,2,192]{3,0,2,1:T(2,128)}), f32[2,320,2,192]{3,0,2,1:T(2,128)S(1)}, u32[]{:S(2)}, u32[]{:S(2)}) async-start(f32[2,320,2,192]{3,0,2,1:T(2,128)} %copy.107), calls=%async_computation | async-start | bytes 2621440 | tf_op jit(solution)/shard_map/all_to_all | solution.py:63
  113.3 185.0 %all-gather.8.cloned.1.call-start = ((), (), s32[]{:S(2)}) async-start(), calls=%async_computation.8 | async-start | bytes 5898240 | tf_op jit(solution)/shard_map/all_gather | solution.py:89
  162.2 5.2 %copy-start.8 = (f32[2,320,2,192]{1,3,2,0:T(8,128)S(1)}, f32[2,320,2,192]{1,3,2,0:T(8,128)}, u32[]{:S(2)}) copy-start(f32[2,320,2,192]{1,3,2,0:T(8,128)} %param.11) | copy-start | bytes 2949124
  163.8 20.8 %all-to-all-start.1 = ((f32[8,80,2,192]{3,1,2,0:T(8,128)}), f32[8,80,2,192]{3,1,2,0:T(8,128)S(1)}, u32[]{:S(2)}, u32[]{:S(2)}) async-start(f32[8,80,2,192]{3,1,2,0:T(8,128)} %copy.110), calls=%async_computation.1 | async-start | bytes 2621440 | tf_op jit(solution)/shard_map/all_to_all | solution.py:69
  167.4 223.1 %all-gather.6.cloned.1.call-start = ((), (), s32[]{:S(2)}) async-start(), calls=%async_computation.7 | async-start | bytes 5898240 | tf_op jit(solution)/shard_map/all_gather | solution.py:85
  298.3 8.3 %copy-start.3 = (f32[2,320,1,192]{1,3,0,2:T(8,128)S(1)}, f32[2,320,1,192]{1,3,0,2:T(8,128)}, u32[]{:S(2)}) copy-start(f32[2,320,1,192]{1,3,0,2:T(8,128)} %copy-done.2) | copy-start | bytes 1474564
  366.9 20.8 %all-to-all-start.5 = ((f32[8,80,2,192]{3,1,2,0:T(8,128)}), f32[8,80,2,192]{3,1,2,0:T(8,128)S(1)}, u32[]{:S(2)}, u32[]{:S(2)}) async-start(f32[8,80,2,192]{3,1,2,0:T(8,128)} %copy.134), calls=%async_computation.5 | async-start | bytes 2621440 | tf_op jit(solution)/shard_map/all_to_all | solution.py:69
  400.6 41.9 %copy-start.4 = (f32[2,320,2,192]{1,3,2,0:T(8,128)S(1)}, f32[2,320,2,192]{1,3,2,0:T(8,128)}, u32[]{:S(2)}) copy-start(f32[2,320,2,192]{1,3,2,0:T(8,128)} %param.10) | copy-start | bytes 2949124
  402.7 43.4 %copy-start.6 = (f32[2,320,1,192]{1,3,0,2:T(8,128)S(1)}, f32[2,320,1,192]{1,3,0,2:T(8,128)}, u32[]{:S(2)}) copy-start(f32[2,320,1,192]{1,3,0,2:T(8,128)} %copy.160) | copy-start | bytes 1474564
  441.8 27.1 %copy-start.1 = (s32[320,192]{0,1:T(8,128)S(1)}, s32[320,192]{0,1:T(8,128)}, u32[]{:S(2)}) copy-start(s32[320,192]{0,1:T(8,128)} %param.7) | copy-start | bytes 737284
  442.5 3.6 copy-start.7
  445.1 22.7 %copy-start.5 = (f32[2,320,2,192]{1,3,0,2:T(8,128)S(1)}, f32[2,320,2,192]{1,3,0,2:T(8,128)}, u32[]{:S(2)}) copy-start(f32[2,320,2,192]{1,3,0,2:T(8,128)} %get-tuple-element.33) | copy-start | bytes 2949124
Sparse Core Ops, SparseCore 0:
  10.7 88.5 all-gather.3
  117.0 84.5 all-gather.7
  298.4 84.9 all-gather.5
where the time goes:
time: 480 us; the launch traced here: 476 us
  blocking collectives  151 us (31%)
  waiting for transfers between devices  134 us (28%)
  matrix products  116 us (24%)
  local copies, waits for them, and re-layouts  36.4 us (8%)
  between operations  17.1 us (4%)
  starting transfers between devices  10.7 us (2%)
  other arithmetic  10.5 us (2%)
    all_gather x1, waiting for transfers between devices, per_device(): lax.all_gather(direction_low, 'rcv', axis=1, tiled=True)  89 us
    dot_general x12, matrix products, contract_time(): return jnp.einsum('tf,frk->trk', table, values, precision=highest)  57 us
    all_to_all x2, blocking collectives, gate(): lax.all_to_all(field, 'freq', split_axis=1, concat_axis=0, tiled=True)  40.3 us
    psum x1, blocking collectives, per_device(): new_gamma = lax.psum(jnp.sum(new_gradient * new_gradient), ('freq', 'rcv'))  39.1 us
    psum x1, blocking collectives, per_device(): gamma = lax.psum(jnp.sum(gradient * gradient), ('freq', 'rcv'))  38.8 us
    dot_general x12, matrix products, contract_back(): return jnp.einsum('tf,trk->frk', table, values, precision=highest)  32.3 us
    all_to_all x2, waiting for transfers between devices, gate(): lax.all_to_all(gated_part, 'freq', split_axis=0, concat_axis=1, tiled=True)  31.3 us
    dot_general x3, matrix products, accumulate(): jnp.einsum('fpnm,fmqk->fpnqk', reflection, piece, preferred_element_type=...  26.4 us
  transfers between devices with their start and end apart: 6, of which 4 were waited for; matrix products, arithmetic and copies ran while one was open for 26% of the time, Pallas kernels for 0%

commit v1 on v0

--- a/solution.py
+++ b/solution.py
@@ -10,6 +10,18 @@
 band_start = 5
 tiny = 1e-06
 highest = lax.Precision.HIGHEST
+
+
+def in_blocks(array, dim, devices):
+    lengths = array.shape
+    blocks = array.reshape(*lengths[:dim], devices, lengths[dim] // devices, *lengths[dim + 1 :])
+    return jnp.moveaxis(blocks, dim, 0)
+
+
+def in_order(blocks, dim):
+    blocks = jnp.moveaxis(blocks, 0, dim)
+    shape = blocks.shape
+    return blocks.reshape(*shape[:dim], shape[dim] * shape[dim + 1], *shape[dim + 2 :])
 
 
 def tables(count):
@@ -60,7 +72,16 @@
     cos_table, sin_table = tables(F)
 
     def gate(field, complement):
-        spread = lax.all_to_all(field, "freq", split_axis=1, concat_axis=0, tiled=True)
+        length, index = (lax.axis_size("freq"), lax.axis_index("freq"))
+        blocks = in_blocks(field, 1, length)
+        done = [blocks[index]]
+        for step in range(1, length):
+            sent = blocks[(index + step) % length]
+            done.append(
+                lax.ppermute(sent, "freq", [(i, (i + step) % length) for i in range(length)])
+            )
+        blocks = jnp.stack(done)[(index - jnp.arange(length)) % length]
+        spread = in_order(blocks, 0)
         share = local_rows // groups
         limits = lax.dynamic_slice_in_dim(starts, position * share, share, 0)
         gated_part = time_gate(

time: 480 us -> 465 us (0.969)
  blocking collectives: 151 us -> 109 us
  waiting for transfers between devices: 134 us -> 146 us
  starting transfers between devices: 10.7 us -> 17 us
  local copies, waits for them, and re-layouts: 36.4 us -> 41.9 us
    all_to_all x2 -> x0, blocking collectives: 40.3 us -> none  [gate(): lax.all_to_all(field, 'freq', split_axis=1, concat_axis=0, tiled=True)]
    ppermute x0 -> x9, waiting for transfers between devices: none -> 35.3 us  [gate(): lax.ppermute(sent, 'freq', [(i, (i + step) % length) for i in range(lengt...]
    all_to_all x1 -> x0, waiting for transfers between devices: 13.3 us -> none  [gate(): lax.all_to_all(field, 'freq', split_axis=1, concat_axis=0, tiled=True)]
    all_to_all x9 -> x0, local copies, waits for them, and re-layouts: 12 us -> none  [gate(): lax.all_to_all(field, 'freq', split_axis=1, concat_axis=0, tiled=True)]
    ppermute x0 -> x9, starting transfers between devices: none -> 9.01 us  [gate(): lax.ppermute(sent, 'freq', [(i, (i + step) % length) for i in range(lengt...]
    all_to_all x2, waiting for transfers between devices: 31.3 us -> 23.5 us  [gate(): lax.all_to_all(gated_part, 'freq', split_axis=0, concat_axis=1, tiled=True)]
    gather x0 -> x3, local copies, waits for them, and re-layouts: none -> 6.44 us  [gate(): blocks = jnp.stack(done)[(index - jnp.arange(length)) % length]]
    unnamed x26 -> x22, local copies, waits for them, and re-layouts: 9.67 us -> 15.1 us
  transfers between devices with their start and end apart: 6 -> 14, of which waited for: 4 -> 11; matrix products, arithmetic and copies ran while one was open for 26% -> 33% of each run, Pallas kernels for 0% -> 0%
where the time goes in v1:
time: 465 us; the launch traced here: 460 us
  waiting for transfers between devices  146 us (31%)
  matrix products  116 us (25%)
  blocking collectives  109 us (23%)
  local copies, waits for them, and re-layouts  41.9 us (9%)
  between operations  17.2 us (4%)
  starting transfers between devices  17 us (4%)
  other arithmetic  13.6 us (3%)
    all_gather x1, waiting for transfers between devices, per_device(): lax.all_gather(direction_low, 'rcv', axis=1, tiled=True)  86.8 us
    dot_general x12, matrix products, contract_time(): return jnp.einsum('tf,frk->trk', table, values, precision=highest)  57.2 us
    psum x1, blocking collectives, per_device(): gamma = lax.psum(jnp.sum(gradient * gradient), ('freq', 'rcv'))  39.2 us
    psum x1, blocking collectives, per_device(): new_gamma = lax.psum(jnp.sum(new_gradient * new_gradient), ('freq', 'rcv'))  37 us
    ppermute x9, waiting for transfers between devices, gate(): lax.ppermute(sent, 'freq', [(i, (i + step) % length) for i in range(lengt...  35.3 us
    dot_general x12, matrix products, contract_back(): return jnp.einsum('tf,trk->frk', table, values, precision=highest)  32.3 us
    dot_general x3, matrix products, accumulate(): jnp.einsum('fpnm,fmqk->fpnqk', reflection, piece, preferred_element_type=...  26.4 us
    all_to_all x2, waiting for transfers between devices, gate(): lax.all_to_all(gated_part, 'freq', split_axis=0, concat_axis=1, tiled=True)  23.5 us
  transfers between devices with their start and end apart: 14, of which 11 were waited for; matrix products, arithmetic and copies ran while one was open for 33% of the time, Pallas kernels for 0%

profile of v1, /device:TPU:0, one launch (start us, length us, event | category | flops | bytes accessed | tf_op | source)
XLA Modules:
  0.0 459.9 jit_solution(3876360536449544174)
XLA Ops:
  12.6 86.8 %all-gather.4.cloned.1.call-done = bf16[2,2560,2,192]{3,2,0,1:T(2,128)(2,1)} async-done(((bf16[2,320,2,192]{3,2,0,1:T(2,128)(2,1)}), bf16[2,2560,2,192]{3,2,0,1:T(2,128)(2,1)}) %all-gather.4.cloned.1.call-update) | async-done | bytes 3932176 | tf_op jit(solution)/shard_map/all_gather | solution.py:97
  99.4 8.1 %fusion.4 = f32[2,2,320,2,192]{2,4,3,1,0:T(8,128)S(1)} fusion(bf16[2,2,320,2560]{3,2,1,0:T(8,128)(2,1)} %param.6, bf16[2,2560,2,192,1]{3,2,0,1,4:T(2,128)(2,1)} %bitcast.228), kind=kOutput, calls=%fused_computation.7 | convolution fusion | flops 2516582400 | bytes 12451840 | tf_op jit(solution)/shard_map/fpnm,fmqk->fpnqk/dot_general | solution.py:93
  113.1 5.5 %collective-permute-done.1 = f32[2,80,2,192]{3,1,2,0:T(8,128)S(1)} collective-permute-done((f32[2,80,2,192]{3,1,2,0:T(8,128)}, f32[2,80,2,192]{3,1,2,0:T(8,128)S(1)}, u32[]{:S(2)}, u32[]{:S(2)}) %collective-permute-start.1) | collective-permute-done | bytes 245792 | tf_op jit(solution)/shard_map/ppermute | solution.py:81
  118.6 4.6 %collective-permute-done.2 = f32[2,80,2,192]{3,1,2,0:T(8,128)S(1)} collective-permute-done((f32[2,80,2,192]{3,1,2,0:T(8,128)}, f32[2,80,2,192]{3,1,2,0:T(8,128)S(1)}, u32[]{:S(2)}, u32[]{:S(2)}) %collective-permute-start.2) | collective-permute-done | bytes 245792 | tf_op jit(solution)/shard_map/ppermute | solution.py:81
  128.3 4.4 fusion.30
  132.7 4.4 fusion.29
  137.1 5.0 %subtract_select_fusion.1 = f32[64,80,192]{2,0,1:T(8,128)S(1)} fusion(f32[64,80,192]{2,0,1:T(8,128)S(1)} %fusion.30, s32[80,192]{1,0:T(8,128)S(1)} %copy.89, f32[8,80,1,192]{3,1,2,0:T(8,128)S(1)} %get-tuple-element.45, f32[8]{0:T(128)S(1)} %add_convert_fusion, f32[64]{0:T(128)S(1)} %iota_multiply_fusion), kind=kOutput, calls=%fused_computation.18 | convolution fusion | flops 97321984 | bytes 8417568 | tf_op jit(solution)/shard_map/tf,frk->trk/dot_general | solution.py:35
  142.2 2.6 fusion.69
  144.8 4.9 %add_select_fusion.1 = f32[64,80,192]{2,0,1:T(8,128)S(1)} fusion(f32[64,80,192]{2,0,1:T(8,128)S(1)} %fusion.29, s32[80,192]{1,0:T(8,128)S(1)} %copy.89, f32[8,80,1,192]{3,1,2,0:T(8,128)S(1)} %get-tuple-element.45, f32[8]{0:T(128)S(1)} %add_convert_fusion, f32[64]{0:T(128)S(1)} %iota_multiply_fusion), kind=kOutput, calls=%fused_computation.17 | convolution fusion | flops 97321984 | bytes 8417568 | tf_op jit(solution)/shard_map/tf,frk->trk/dot_general | solution.py:35
  149.7 2.7 fusion.27
  152.4 2.8 fusion.66
  155.2 2.7 fusion.25
  159.5 3.5 all-to-all-start
  163.1 2.2 multiply_reduce_fusion.2
  165.2 15.4 %all-to-all-done = f32[8,80,2,192]{3,1,2,0:T(8,128)S(1)} async-done(((f32[8,80,2,192]{3,1,2,0:T(8,128)}), f32[8,80,2,192]{3,1,2,0:T(8,128)S(1)}, u32[]{:S(2)}, u32[]{:S(2)}) %all-to-all-start) | async-done | bytes 983072 | tf_op jit(solution)/shard_map/all_to_all | solution.py:90
  181.6 2.8 copy.103
  184.4 39.2 %all-reduce = (f32[]{:T(128)}, f32[]{:T(128)}) all-reduce(f32[]{:T(128)} %multiply_reduce_fusion.2, f32[]{:T(128)} %multiply_reduce_fusion), channel_id=1, replica_groups=mesh['freq'=4,'rcv'=8] {'freq','rcv'}, use_global_device_ids=true, to_apply=%region_1.0 | all-reduce | flops 2 | bytes 16 | tf_op jit(solution)/shard_map/psum | solution.py:99
  226.6 2.3 collective-permute-start.4
  230.7 5.0 %collective-permute-done.3 = f32[2,80,2,192]{3,1,2,0:T(8,128)S(1)} collective-permute-done((f32[2,80,2,192]{3,1,2,0:T(8,128)S(1)}, f32[2,80,2,192]{3,1,2,0:T(8,128)S(1)}, u32[]{:S(2)}, u32[]{:S(2)}) %collective-permute-start.3) | collective-permute-done | bytes 245792 | tf_op jit(solution)/shard_map/ppermute | solution.py:81
  237.5 5.9 %collective-permute-done.5 = f32[2,80,2,192]{3,1,2,0:T(8,128)S(1)} collective-permute-done((f32[2,80,2,192]{3,1,2,0:T(8,128)S(1)}, f32[2,80,2,192]{3,1,2,0:T(8,128)S(1)}, u32[]{:S(2)}, u32[]{:S(2)}) %collective-permute-start.5) | collective-permute-done | bytes 245792 | tf_op jit(solution)/shard_map/ppermute | solution.py:81
  244.7 3.0 gather_fusion.1
  249.0 4.4 fusion.32
  253.5 4.4 fusion.31
  257.9 5.1 %subtract_select_fusion = f32[64,80,192]{2,0,1:T(8,128)S(1)} fusion(f32[64,80,192]{2,0,1:T(8,128)S(1)} %fusion.32, s32[80,192]{1,0:T(8,128)S(1)} %copy.89, f32[8,80,1,192]{3,1,2,0:T(8,128)S(1)} %get-tuple-element.39, f32[8]{0:T(128)S(1)} %add_convert_fusion, f32[64]{0:T(128)S(1)} %iota_multiply_fusion), kind=kOutput, calls=%fused_computation.16 | convolution fusion | flops 97321984 | bytes 8417568 | tf_op jit(solution)/shard_map/tf,frk->trk/dot_general | solution.py:35
  262.9 2.6 fusion.63
  265.6 4.9 %add_select_fusion = f32[64,80,192]{2,0,1:T(8,128)S(1)} fusion(f32[64,80,192]{2,0,1:T(8,128)S(1)} %fusion.31, s32[80,192]{1,0:T(8,128)S(1)} %copy.89, f32[8,80,1,192]{3,1,2,0:T(8,128)S(1)} %get-tuple-element.39, f32[8]{0:T(128)S(1)} %add_convert_fusion, f32[64]{0:T(128)S(1)} %iota_multiply_fusion), kind=kOutput, calls=%fused_computation.15 | convolution fusion | flops 97321984 | bytes 8417568 | tf_op jit(solution)/shard_map/tf,frk->trk/dot_general | solution.py:35
  270.5 2.6 fusion.23
  273.1 2.8 fusion.60
  275.9 2.6 fusion.21
  278.8 13.2 %all_to_all.36 = bf16[8,80,2,192]{3,1,2,0:T(8,128)(2,1)S(1)} all-to-all(bf16[8,80,2,192]{3,1,2,0:T(8,128)(2,1)S(1)} %copy.105), channel_id=1, replica_groups=mesh['freq'=4,'rcv'=8] {'freq'}, dimensions={0} | all-to-all | bytes 983040 | tf_op jit(solution)/shard_map/all_to_all | solution.py:90
  293.6 8.1 %fusion.2 = f32[2,2,320,2,192]{2,4,3,1,0:T(8,128)S(1)} fusion(bf16[2,2,320,2560]{3,2,1,0:T(8,128)(2,1)} %param.6, bf16[2,2560,2,192,1]{3,2,0,1,4:T(2,128)(2,1)} %bitcast.226), kind=kOutput, calls=%fused_computation.5 | convolution fusion | flops 2516582400 | bytes 12451840 | tf_op jit(solution)/shard_map/fpnm,fmqk->fpnqk/dot_general | solution.py:93
  302.7 2.2 copy.114
  310.1 6.9 %collective-permute-done.6 = f32[2,80,2,192]{3,1,2,0:T(8,128)S(1)} collective-permute-done((f32[2,80,2,192]{3,1,2,0:T(8,128)S(1)}, f32[2,80,2,192]{3,1,2,0:T(8,128)S(1)}, u32[]{:S(2)}, u32[]{:S(2)}) %collective-permute-start.6) | collective-permute-done | bytes 245792 | tf_op jit(solution)/shard_map/ppermute | solution.py:81
  318.3 4.3 collective-permute-done.8
  325.8 4.4 fusion.34
  330.2 4.4 fusion.33
  334.6 5.5 %subtract_multiply_fusion = f32[64,80,192]{2,0,1:T(8,128)S(1)} fusion(f32[64,80,192]{2,0,1:T(8,128)S(1)} %fusion.34, s32[80,192]{1,0:T(8,128)S(1)} %copy.89, f32[8,80,1,192]{3,1,2,0:T(8,128)S(1)} %get-tuple-element.33, f32[8]{0:T(128)S(1)} %add_convert_fusion, f32[64]{0:T(128)S(1)} %iota_multiply_fusion), kind=kOutput, calls=%fused_computation.13 | convolution fusion | flops 99288064 | bytes 8417568 | tf_op jit(solution)/shard_map/tf,frk->trk/dot_general | solution.py:35
  340.1 2.6 fusion.57
  342.8 5.3 %add_multiply_fusion = f32[64,80,192]{2,0,1:T(8,128)S(1)} fusion(f32[64,80,192]{2,0,1:T(8,128)S(1)} %fusion.33, s32[80,192]{1,0:T(8,128)S(1)} %copy.89, f32[8,80,1,192]{3,1,2,0:T(8,128)S(1)} %get-tuple-element.33, f32[8]{0:T(128)S(1)} %add_convert_fusion, f32[64]{0:T(128)S(1)} %iota_multiply_fusion), kind=kOutput, calls=%fused_computation.12 | convolution fusion | flops 99288064 | bytes 8417568 | tf_op jit(solution)/shard_map/tf,frk->trk/dot_general | solution.py:35
  348.1 2.7 fusion.19
  350.8 2.8 fusion.54
  353.6 2.7 fusion.17
  357.8 4.3 all-to-all-start.2
  363.6 2.8 copy.101
  371.9 8.1 %all-to-all-done.2 = f32[8,80,2,192]{3,1,2,0:T(8,128)} async-done(((f32[8,80,2,192]{3,1,2,0:T(8,128)}), f32[8,80,2,192]{3,1,2,0:T(8,128)}, u32[]{:S(2)}, u32[]{:S(2)}) %all-to-all-start.2) | async-done | bytes 983072 | tf_op jit(solution)/shard_map/all_to_all | solution.py:90
  383.1 19.3 %psum.31 = f32[2,2,192]{2,0,1:T(2,128)S(1)} all-reduce(f32[2,2,192]{2,0,1:T(2,128)S(1)} %pad_maximum_fusion.8), channel_id=1, replica_groups=mesh['freq'=4,'rcv'=8] {'rcv'}, use_global_device_ids=true, to_apply=%region_8.9 | all-reduce | flops 768 | bytes 6144 | tf_op jit(solution)/shard_map/psum | solution.py:122
  402.4 10.2 %fusion.9 = f32[2,2,320,2,192]{2,4,1,3,0:T(8,128)S(1)} fusion(bf16[2,2,320,2560]{3,2,1,0:T(8,128)(2,1)} %param.6, bf16[2,2560,2,192,1]{3,2,0,1,4:T(2,128)(2,1)} %bitcast.227), kind=kOutput, calls=%fused_computation.29 | convolution fusion | flops 2516582400 | bytes 12451840 | tf_op jit(solution)/shard_map/fpnm,fmqk->fpnqk/dot_general | solution.py:93
  414.2 37.0 %psum.30 = f32[]{:T(128)} all-reduce(f32[]{:T(128)} %multiply_reduce_fusion.1), channel_id=1, replica_groups=mesh['freq'=4,'rcv'=8] {'freq','rcv'}, use_global_device_ids=true, to_apply=%region_5.6 | all-reduce | flops 1 | bytes 8 | tf_op jit(solution)/shard_map/psum | solution.py:108
  (95 shorter events, 52.6 us)
Async XLA Ops:
  7.2 5.4 %copy-start = (s32[320,192]{0,1:T(8,128)S(1)}, s32[320,192]{0,1:T(8,128)}, u32[]{:S(2)}) copy-start(s32[320,192]{0,1:T(8,128)} %param.7) | copy-start | bytes 737284
  7.2 3.4 copy-start.5
  7.2 92.2 %all-gather.4.cloned.1.call-start = ((), (), s32[]{:S(2)}) async-start(), calls=%async_computation.3 | async-start | bytes 5898240 | tf_op jit(solution)/shard_map/all_gather | solution.py:97
  10.5 283.1 %all-gather.8.cloned.1.call-start = ((), (), s32[]{:S(2)}) async-start(), calls=%async_computation.5 | async-start | bytes 5898240 | tf_op jit(solution)/shard_map/all_gather | solution.py:110
  109.0 9.6 %collective-permute-start.1 = (f32[2,80,2,192]{3,1,2,0:T(8,128)}, f32[2,80,2,192]{3,1,2,0:T(8,128)S(1)}, u32[]{:S(2)}, u32[]{:S(2)}) collective-permute-start(f32[2,80,2,192]{3,1,2,0:T(8,128)} %bitcast.193), channel_id=1, source_target_pairs={{0,16},{8,24},{16,0},{24,8},{1,17},{9,25},{17,1},{25,9},{2,18},{10... | collective-permute-start | bytes 737288 | tf_op jit(solution)/shard_map/ppermute | solution.py:81
  111.3 12.0 %collective-permute-start.2 = (f32[2,80,2,192]{3,1,2,0:T(8,128)}, f32[2,80,2,192]{3,1,2,0:T(8,128)S(1)}, u32[]{:S(2)}, u32[]{:S(2)}) collective-permute-start(f32[2,80,2,192]{3,1,2,0:T(8,128)} %bitcast.192), channel_id=1, source_target_pairs={{0,24},{8,0},{16,8},{24,16},{1,25},{9,1},{17,9},{25,17},{2,26},{10... | collective-permute-start | bytes 737288 | tf_op jit(solution)/shard_map/ppermute | solution.py:81
  112.0 11.3 %collective-permute-start = (f32[2,80,2,192]{3,1,2,0:T(8,128)}, f32[2,80,2,192]{3,1,2,0:T(8,128)}, u32[]{:S(2)}, u32[]{:S(2)}) collective-permute-start(f32[2,80,2,192]{3,1,2,0:T(8,128)} %bitcast.194), channel_id=1, source_target_pairs={{0,8},{8,16},{16,24},{24,0},{1,9},{9,17},{17,25},{25,1},{2,10},{10... | collective-permute-start | bytes 737288 | tf_op jit(solution)/shard_map/ppermute | solution.py:81
  123.3 0.7 copy-start.6
  159.5 21.2 %all-to-all-start = ((f32[8,80,2,192]{3,1,2,0:T(8,128)}), f32[8,80,2,192]{3,1,2,0:T(8,128)S(1)}, u32[]{:S(2)}, u32[]{:S(2)}) async-start(f32[8,80,2,192]{3,1,2,0:T(8,128)} %copy.99), calls=%async_computation | async-start | bytes 2621440 | tf_op jit(solution)/shard_map/all_to_all | solution.py:90
  163.0 239.4 %all-gather.6.cloned.1.call-start = ((), (), s32[]{:S(2)}) async-start(), calls=%async_computation.4 | async-start | bytes 5898240 | tf_op jit(solution)/shard_map/all_gather | solution.py:106
  224.9 1.3 copy-start.4
  226.5 9.2 %collective-permute-start.3 = (f32[2,80,2,192]{3,1,2,0:T(8,128)S(1)}, f32[2,80,2,192]{3,1,2,0:T(8,128)S(1)}, u32[]{:S(2)}, u32[]{:S(2)}) collective-permute-start(f32[2,80,2,192]{3,1,2,0:T(8,128)S(1)} %get-tuple-element.44), channel_id=1, source_target_pairs={{0,8},{8,16},{16,24},{24,0},{1,9},{9,17},{17,25},{25,1},{2,10},{10... | collective-permute-start | bytes 737288 | tf_op jit(solution)/shard_map/ppermute | solution.py:81
  226.6 10.9 %collective-permute-start.4 = (f32[2,80,2,192]{3,1,2,0:T(8,128)S(1)}, f32[2,80,2,192]{3,1,2,0:T(8,128)S(1)}, u32[]{:S(2)}, u32[]{:S(2)}) collective-permute-start(f32[2,80,2,192]{3,1,2,0:T(8,128)S(1)} %get-tuple-element.43), channel_id=1, source_target_pairs={{0,16},{8,24},{16,0},{24,8},{1,17},{9,25},{17,1},{25,9},{2,18},{10... | collective-permute-start | bytes 737288 | tf_op jit(solution)/shard_map/ppermute | solution.py:81
  228.9 14.5 %collective-permute-start.5 = (f32[2,80,2,192]{3,1,2,0:T(8,128)S(1)}, f32[2,80,2,192]{3,1,2,0:T(8,128)S(1)}, u32[]{:S(2)}, u32[]{:S(2)}) collective-permute-start(f32[2,80,2,192]{3,1,2,0:T(8,128)S(1)} %get-tuple-element.42), channel_id=1, source_target_pairs={{0,24},{8,0},{16,8},{24,16},{1,25},{9,1},{17,9},{25,17},{2,26},{10... | collective-permute-start | bytes 737288 | tf_op jit(solution)/shard_map/ppermute | solution.py:81
  307.6 9.4 %collective-permute-start.6 = (f32[2,80,2,192]{3,1,2,0:T(8,128)S(1)}, f32[2,80,2,192]{3,1,2,0:T(8,128)S(1)}, u32[]{:S(2)}, u32[]{:S(2)}) collective-permute-start(f32[2,80,2,192]{3,1,2,0:T(8,128)S(1)} %bitcast.221), channel_id=1, source_target_pairs={{0,8},{8,16},{16,24},{24,0},{1,9},{9,17},{17,25},{25,1},{2,10},{10... | collective-permute-start | bytes 737288 | tf_op jit(solution)/shard_map/ppermute | solution.py:81
  307.7 10.6 %collective-permute-start.7 = (f32[2,80,2,192]{3,1,2,0:T(8,128)S(1)}, f32[2,80,2,192]{3,1,2,0:T(8,128)S(1)}, u32[]{:S(2)}, u32[]{:S(2)}) collective-permute-start(f32[2,80,2,192]{3,1,2,0:T(8,128)S(1)} %bitcast.222), channel_id=1, source_target_pairs={{0,16},{8,24},{16,0},{24,8},{1,17},{9,25},{17,1},{25,9},{2,18},{10... | collective-permute-start | bytes 737288 | tf_op jit(solution)/shard_map/ppermute | solution.py:81
  308.2 14.4 %collective-permute-start.8 = (f32[2,80,2,192]{3,1,2,0:T(8,128)S(1)}, f32[2,80,2,192]{3,1,2,0:T(8,128)S(1)}, u32[]{:S(2)}, u32[]{:S(2)}) collective-permute-start(f32[2,80,2,192]{3,1,2,0:T(8,128)S(1)} %bitcast.223), channel_id=1, source_target_pairs={{0,24},{8,0},{16,8},{24,16},{1,25},{9,1},{17,9},{25,17},{2,26},{10... | collective-permute-start | bytes 737288 | tf_op jit(solution)/shard_map/ppermute | solution.py:81
  356.3 5.8 %copy-start.2 = (f32[2,320,2,192]{1,3,2,0:T(8,128)S(1)}, f32[2,320,2,192]{1,3,2,0:T(8,128)}, u32[]{:S(2)}) copy-start(f32[2,320,2,192]{1,3,2,0:T(8,128)} %param.10) | copy-start | bytes 2949124
  357.8 22.1 %all-to-all-start.2 = ((f32[8,80,2,192]{3,1,2,0:T(8,128)}), f32[8,80,2,192]{3,1,2,0:T(8,128)}, u32[]{:S(2)}, u32[]{:S(2)}) async-start(f32[8,80,2,192]{3,1,2,0:T(8,128)} %copy.121), calls=%async_computation.2 | async-start | bytes 2621440 | tf_op jit(solution)/shard_map/all_to_all | solution.py:90
  412.6 39.4 %copy-start.3 = (f32[2,320,2,192]{1,3,2,0:T(8,128)S(1)}, f32[2,320,2,192]{1,3,2,0:T(8,128)}, u32[]{:S(2)}) copy-start(f32[2,320,2,192]{1,3,2,0:T(8,128)} %param.10) | copy-start | bytes 2949124
  451.2 1.9 copy-start.1
Sparse Core Ops, SparseCore 0:
  10.8 88.5 all-gather.3
  102.2 84.1 all-gather.7
  293.7 84.1 all-gather.5
